TPU v7x, 32 devices: a whole 2x2x4 slice. The times are simulated.
32 devices in a mesh: grp: 8 (over z, y), rep: 2 (over core), tp: 2 (over x).
Axes of the slice: x: 2, y: 2, z: 4, core: 2. Of those that a mesh axis runs over, the one named last changes fastest.
Arguments:
- hidden: bfloat16 [8, 768, 8192], P('grp', 'rep'), may hold values from -6 to 6
- decode_hidden: bfloat16 [8, 2, 2, 32, 8192], P('grp', 'rep'), may hold values from -6 to 6
- norm_gain: bfloat16 [8192], replicated, may hold values from 0.25 to 1.75
- qkv_weight: bfloat16 [8192, 10240], P('grp', 'tp'), may hold values from -0.0625 to 0.0625
- qkv_bias: bfloat16 [10240], P('tp'), may hold values from -32 to 32
- lengths: int32 [8], replicated, may hold values from 12 to 768, as said below
Outputs:
- prefill_out: bfloat16 [8, 768, 8192], P('grp', 'rep', 'tp')
- decode_out: bfloat16 [8, 2, 2, 32, 8192], P('grp', 'rep', None, None, 'tp')
Inputs may be any that keep to these rules, and one draw needn't show every extreme that they name: `lengths`: some prompt is 768 tokens long.
All inputs are finite; a program needn't handle non-finite values.
Results may differ from a plain program's by a relative error of at most 0.012.
The roundings to bfloat16 on the way count: a program that leaves them out, or rounds other values in their place, can miss the bound.
Values may be sent and summed in bfloat16 or wider, within the bound.
A program may use at most 256 MiB of HBM per device.

v0:
```python
import jax
import jax.numpy as jnp
from jax import lax
from jax.sharding import PartitionSpec as P

HD = 128
QPK = 8
STEPS = 4
THETA = 1000000.0
EPSILON = 1e-06
NEGATIVE = -1e30


def shifted(block, axis, distance):
    devices = range(lax.axis_size(axis))
    route = [((i - distance) % len(devices), i) for i in devices]
    return lax.ppermute(block, axis, route)


def normalize(row_block, gain_row):
    widened = row_block.astype(jnp.float32)
    factor = lax.rsqrt(jnp.mean(widened * widened, axis=-1, keepdims=True) + EPSILON)
    return (widened * factor * gain_row.astype(jnp.float32)).astype(jnp.bfloat16)


def rope_tables(positions, head_size):
    half_size = head_size // 2
    frequency = THETA ** (-(jnp.arange(half_size, dtype=jnp.float32) * 2.0 / head_size))
    angle = positions.astype(jnp.float32)[:, None] * frequency[None, :]
    return (jnp.cos(angle), jnp.sin(angle))


def rotate(vector, cosine, sine_part):
    half_size = vector.shape[-1] // 2
    first_half = vector[..., :half_size]
    second = vector[..., half_size:]
    return jnp.concatenate(
        [first_half * cosine - second * sine_part, second * cosine + first_half * sine_part],
        axis=-1,
    )


def masked_max(scores, allowed):
    return jnp.max(jnp.where(allowed, scores, NEGATIVE), axis=-1, keepdims=True)


def combine_values(weight_matrix, value_matrix):
    return jnp.einsum(
        "aprk,kaz->rapz",
        weight_matrix.astype(jnp.bfloat16),
        value_matrix,
        preferred_element_type=jnp.float32,
    )


def pair_scores(query_matrix, key_matrix_rows, score_scale):
    return (
        jnp.einsum(
            "wjro,ujo->jrwu", query_matrix, key_matrix_rows, preferred_element_type=jnp.float32
        )
        * score_scale
    )


def decode_pair(
    query_matrix,
    own_keys,
    own_values,
    prompt_keys,
    prompt_values,
    valid_len,
    local_allowed,
    score_scale,
):
    key_slot_index = jnp.arange(prompt_keys.shape[0], dtype=jnp.int32)
    prompt_allowed = (key_slot_index < valid_len)[None, None, None, :]
    far_scores = pair_scores(query_matrix, prompt_keys, score_scale)
    near_scores = pair_scores(query_matrix, own_keys, score_scale)
    highest = jnp.maximum(
        masked_max(far_scores, prompt_allowed), masked_max(near_scores, local_allowed)
    )
    far_exp = jnp.where(prompt_allowed, jnp.exp(far_scores - highest), 0.0)
    near_exp = jnp.where(local_allowed, jnp.exp(near_scores - highest), 0.0)
    running = jnp.sum(far_exp, axis=-1, keepdims=True) + jnp.sum(near_exp, axis=-1, keepdims=True)
    return combine_values(far_exp / running, prompt_values) + combine_values(
        near_exp / running, own_values
    )


def on_device(hidden, decode_hidden, norm_gain, qkv_weight, qkv_bias, lengths):
    prompt_count = lax.axis_size("grp")
    rep_count = lax.axis_size("rep")
    half_cycle = prompt_count // 2
    grp_here = lax.axis_index("grp")
    rep_here = lax.axis_index("rep")
    span_rows = hidden.shape[1]
    model_width = hidden.shape[2]
    head_block = (QPK + 2) * HD
    heads_here = qkv_bias.shape[0] // head_block
    decode_rows = decode_hidden.shape[3]
    score_scale = HD ** (-0.5)
    prefill_normed = normalize(hidden[0], norm_gain)
    decode_normed = normalize(decode_hidden.reshape(2 * decode_rows, model_width), norm_gain)
    normed = jnp.concatenate([prefill_normed, decode_normed], axis=0)
    share_cols = qkv_weight.shape[1] // rep_count
    own_cols = lax.dynamic_slice_in_dim(qkv_weight, rep_here * share_cols, share_cols, 1)
    columns = lax.all_gather(own_cols, "grp", axis=0, tiled=True)
    complete = lax.all_gather(columns, "rep", axis=1, tiled=True)
    projected = jnp.dot(normed, complete, preferred_element_type=jnp.float32)
    projected = (projected + qkv_bias.astype(jnp.float32)).reshape(
        normed.shape[0], heads_here, QPK + 2, HD
    )
    index_table = jnp.arange(prompt_count, dtype=jnp.int32)

    def length_of(prompt):
        return jnp.sum(jnp.where(index_table == prompt, lengths, 0))

    own_len = length_of(grp_here)
    far_len = length_of((grp_here + half_cycle) % prompt_count)
    row_position = rep_here * span_rows + jnp.arange(span_rows, dtype=jnp.int32)
    local_ids = jnp.arange(decode_rows, dtype=jnp.int32)
    step_ids = local_ids % STEPS
    sample_ids = local_ids // STEPS
    positions = jnp.concatenate([row_position, own_len + step_ids, far_len + step_ids])
    cosine, sine_part = rope_tables(positions, HD)
    query_matrix = rotate(
        projected[:, :, :QPK], cosine[:, None, None, :], sine_part[:, None, None, :]
    ).astype(jnp.bfloat16)
    key_matrix_rows = rotate(
        projected[:, :, QPK], cosine[:, None, :], sine_part[:, None, :]
    ).astype(jnp.bfloat16)
    value_matrix = projected[:, :, QPK + 1].astype(jnp.bfloat16)
    cache_keys, cache_values = (
        lax.all_gather(key_matrix_rows[:span_rows], "rep", axis=0, tiled=True),
        lax.all_gather(value_matrix[:span_rows], "rep", axis=0, tiled=True),
    )
    key_pos = jnp.arange(cache_keys.shape[0], dtype=jnp.int32)
    allowed = ((key_pos[None, :] <= row_position[:, None]) & (key_pos[None, :] < own_len))[
        None, None
    ]
    scores = pair_scores(query_matrix[:span_rows], cache_keys, score_scale)
    highest = masked_max(scores, allowed)
    exponent = jnp.where(allowed, jnp.exp(scores - highest), 0.0)
    weight_matrix = exponent / jnp.sum(exponent, axis=-1, keepdims=True)
    attended = combine_values(weight_matrix, cache_values)
    prefill_out = attended.astype(jnp.bfloat16).reshape(1, span_rows, heads_here * QPK * HD)
    decode_queries = query_matrix[span_rows:].reshape(2, decode_rows, heads_here, QPK, HD)
    decode_keys = key_matrix_rows[span_rows:].reshape(2, decode_rows, heads_here, HD)
    decode_values = value_matrix[span_rows:].reshape(2, decode_rows, heads_here, HD)
    local_allowed = (
        (sample_ids[None, :] == sample_ids[:, None]) & (step_ids[None, :] <= step_ids[:, None])
    )[None, None]
    near_out = decode_pair(
        decode_queries[0],
        decode_keys[0],
        decode_values[0],
        cache_keys,
        cache_values,
        own_len,
        local_allowed,
        score_scale,
    )
    far_keys, far_values = shifted((cache_keys, cache_values), "grp", half_cycle)
    far_out = decode_pair(
        decode_queries[1],
        decode_keys[1],
        decode_values[1],
        far_keys,
        far_values,
        far_len,
        local_allowed,
        score_scale,
    )
    decode_out = (
        jnp.stack([near_out, far_out])
        .astype(jnp.bfloat16)
        .reshape(1, 1, 2, decode_rows, heads_here * QPK * HD)
    )
    return (prefill_out, decode_out)


def solution(mesh):
    return jax.shard_map(
        on_device,
        mesh=mesh,
        in_specs=(
            P("grp", "rep", None),
            P("grp", "rep", None, None, None),
            P(),
            P("grp", "tp"),
            P("tp"),
            P(),
        ),
        out_specs=(P("grp", "rep", "tp"), P("grp", "rep", None, None, "tp")),
        check_vma=False,
    )
```

profile of v0, /device:TPU:0, one launch (start us, length us, event | category | flops | bytes accessed | tf_op | source)
XLA Modules:
  0.0 1132.9 jit_solution(10912499802913706107)
XLA Ops:
  7.2 5.1 constant_dynamic-slice_fusion
  12.4 797.8 %all-gather.4.cloned.1.call-done = bf16[8192,2560]{1,0:T(8,128)(2,1)} async-done(((bf16[1024,2560]{1,0:T(8,128)(2,1)}), bf16[8192,2560]{1,0:T(8,128)(2,1)}) %all-gather.4.cloned.1.call-update) | async-done | bytes 41943056 | tf_op jit(solution)/shard_map/all_gather | solution.py:107
  815.8 4.9 fusion.9
  823.6 12.1 %fusion.11 = bf16[384,8192]{1,0:T(8,128)(2,1)} fusion(bf16[1,384,8192]{2,1,0:T(8,128)(2,1)} %param.6, f32[8192]{0:T(1024)S(1)} %convert_element_type.70, f32[384]{0:T(512)S(1)} %add_rsqrt_fusion), kind=kLoop, calls=%fused_computation.16 | loop fusion | flops 12582912 | bytes 12617216 | tf_op jit(solution)/shard_map/convert_element_type | solution.py:23
  835.6 95.3 %all-gather.6.cloned.1.call-done = bf16[8192,5120]{1,0:T(8,128)(2,1)} async-done(((bf16[8192,2560]{1,0:T(8,128)(2,1)}), bf16[8192,5120]{1,0:T(8,128)(2,1)}) %all-gather.6.cloned.1.call-update) | async-done | bytes 83886096 | tf_op jit(solution)/shard_map/all_gather | solution.py:108
  931.0 47.5 %fusion.16 = f32[448,5120]{1,0:T(8,128)} fusion(bf16[8192,5120]{1,0:T(8,128)(2,1)} %all-gather.6.cloned.1.call-done, bf16[64,8192]{1,0:T(8,128)(2,1)S(1)} %fusion.32, bf16[384,8192]{1,0:T(8,128)(2,1)} %fusion.11, f32[5120]{0:T(1024)S(1)} %convert_element_type.76), kind=kOutput, calls=%fused_computation.24 | convolution fusion | flops 37597937664 | bytes 100421632 | tf_op jit(solution)/shard_map/dot_general | solution.py:109
  978.5 10.8 copy.20
  990.6 8.8 fusion.92
  999.4 3.1 copy.59
  1004.2 2.5 all_gather.15
  1006.7 6.5 copy.56
  1013.2 6.5 copy.57
  1019.7 6.3 add_convert_fusion
  1029.0 1.9 fusion.25
  1030.9 2.7 collective-permute-start.1
  1033.6 26.4 %fusion.93 = (f32[4,8,384]{2,1,0:T(8,128)S(1)}, f32[4,8,384,768]{2,3,1,0:T(8,128)}) fusion(pred[384,768]{0,1:T(8,128)(4,1)} %fusion.40, bf16[768,4,128]{2,0,1:T(8,128)(2,1)} %all_gather.15, bf16[448,4,8,64]{3,0,2,1:T(8,128)(2,1)} %copy-done.2, bf16[448,4,8,64]{3,0,2,1:T(8,128)(2,1)} %copy-done.1), kind=kOutput, calls=%fused_computation.139 | convolution fusion | flops 4901044736 | bytes 54640640 | tf_op jit(solution)/shard_map/sub | solution.py:143
  1061.1 2.5 all-gather
  1063.6 15.2 %fusion.30 = bf16[4,128,8,384]{3,1,2,0:T(8,128)(2,1)} fusion(f32[4,8,384,768]{2,3,1,0:T(8,128)} %get-tuple-element.19, f32[4,8,384]{2,1,0:T(8,128)S(1)} %get-tuple-element.18, bf16[768,4,1,128]{0,3,1,2:T(8,128)(2,1)} %all-gather), kind=kOutput, calls=%fused_computation.45 | convolution fusion | flops 2436366336 | bytes 41730048 | tf_op jit(solution)/shard_map/aprk,kaz->rapz/dot_general | solution.py:48
  1078.8 4.6 copy.34
  1083.5 1.8 select_reduce_fusion.1
  1087.8 2.1 fusion.33
  1091.4 1.8 fusion.22
  1095.5 27.3 %collective-permute-done = bf16[768,4,128]{0,2,1:T(8,128)(2,1)} collective-permute-done((bf16[768,4,128]{0,2,1:T(8,128)(2,1)}, bf16[768,4,128]{0,2,1:T(8,128)(2,1)}, u32[]{:S(2)}, u32[]{:S(2)}) %collective-permute-start) | collective-permute-done | bytes 786464 | tf_op jit(solution)/shard_map/ppermute | solution.py:17
  1122.9 2.2 fusion.42
  (73 shorter events, 22.6 us)
Async XLA Ops:
  7.2 803.1 %all-gather.4.cloned.1.call-start = ((), (), s32[]{:S(2)}) async-start(), calls=%async_computation | async-start | bytes 47185920 | tf_op jit(solution)/shard_map/all_gather | solution.py:107
  12.4 918.6 %all-gather.6.cloned.1.call-start = ((), (), s32[]{:S(2)}) async-start(), calls=%async_computation.1 | async-start | bytes 125829120 | tf_op jit(solution)/shard_map/all_gather | solution.py:108
  810.2 0.7 copy-start.10
  810.2 1.2 copy-start.7
  810.2 1.6 copy-start.11
  810.2 1.7 copy-start.13
  990.6 8.8 copy-start
  1003.2 0.8 copy-start.3
  1003.2 1.0 copy-start.5
  1026.1 1.8 copy-start.1
  1026.1 2.9 copy-start.2
  1030.9 60.5 %collective-permute-start.1 = (bf16[768,4,128]{2,0,1:T(8,128)(2,1)}, bf16[768,4,128]{2,0,1:T(8,128)(2,1)}, u32[]{:S(2)}, u32[]{:S(2)}) collective-permute-start(bf16[768,4,128]{2,0,1:T(8,128)(2,1)} %all_gather.15), channel_id=1, source_target_pairs={{16,0},{20,4},{24,8},{28,12},{0,16},{4,20},{8,24},{12,28},{17,1},{... | collective-permute-start | bytes 2359304 | tf_op jit(solution)/shard_map/ppermute | solution.py:17
  1078.8 4.6 copy-start.9
  1083.5 2.9 copy-start.4
  1083.5 2.9 copy-start.6
  1085.2 37.6 %collective-permute-start = (bf16[768,4,128]{0,2,1:T(8,128)(2,1)}, bf16[768,4,128]{0,2,1:T(8,128)(2,1)}, u32[]{:S(2)}, u32[]{:S(2)}) collective-permute-start(bf16[768,4,128]{0,2,1:T(8,128)(2,1)} %bitcast.4), channel_id=1, source_target_pairs={{16,0},{20,4},{24,8},{28,12},{0,16},{4,20},{8,24},{12,28},{17,1},{... | collective-permute-start | bytes 2359304 | tf_op jit(solution)/shard_map/ppermute | solution.py:17
  1087.8 3.6 copy-start.12
  1089.9 3.4 copy-start.8
Sparse Core Ops, SparseCore 0:
  12.5 797.6 all-gather.3
  811.8 119.1 all-gather.5
where the time goes:
time: 1130 us
  waiting for transfers between devices  921 us (82%)
  matrix products  103 us (9%)
  local copies, waits for them, and re-layouts  53.4 us (5%)
  other arithmetic  33.8 us (3%)
  between operations  14.4 us (1%)
    all_gather x1, waiting for transfers between devices, on_device(): columns = lax.all_gather(own_cols, 'grp', axis=0, tiled=True)  798 us
    all_gather x1, waiting for transfers between devices, on_device(): complete = lax.all_gather(columns, 'rep', axis=1, tiled=True)  95.3 us
    dot_general x1, matrix products, on_device(): projected = jnp.dot(normed, complete, preferred_element_type=jnp.float32)  47.5 us
    ppermute x2, waiting for transfers between devices, shifted(): return lax.ppermute(block, axis, route)  27.4 us
    sub x1, matrix products, on_device(): exponent = jnp.where(allowed, jnp.exp(scores - highest), 0.0)  26.4 us
    unnamed x32, local copies, waits for them, and re-layouts  22.7 us
  transfers between devices with their start and end apart: 4, of which 3 were waited for; matrix products, arithmetic and copies ran while one was open for 7% of the time, Pallas kernels for 0%

commit v1 on v0

--- a/solution.py
+++ b/solution.py
@@ -2,6 +2,7 @@
 import jax.numpy as jnp
 from jax import lax
 from jax.sharding import PartitionSpec as P
+from jax.lax import axis_index, axis_size, ppermute
 
 HD = 128
 QPK = 8
@@ -104,7 +105,23 @@
     normed = jnp.concatenate([prefill_normed, decode_normed], axis=0)
     share_cols = qkv_weight.shape[1] // rep_count
     own_cols = lax.dynamic_slice_in_dim(qkv_weight, rep_here * share_cols, share_cols, 1)
-    columns = lax.all_gather(own_cols, "grp", axis=0, tiled=True)
+
+    def turn_modes(matrix):
+        mesh_ax = "grp"
+        n_blocks = axis_size(mesh_ax)
+        fields = list(map(lambda j: (j, (j + 1) % n_blocks), range(n_blocks)))
+        rows = list(map(lambda j: (j, (j - 1) % n_blocks), range(n_blocks)))
+        mid_arr, earlier = ([matrix], [matrix])
+        for _ in range(n_blocks // 2):
+            mid_arr.append(ppermute(mid_arr[-1], axis_name=mesh_ax, perm=fields))
+        for _ in range((n_blocks - 1) // 2):
+            earlier.append(ppermute(earlier[-1], axis_name=mesh_ax, perm=rows))
+        arr_out = jnp.concatenate([*mid_arr[::-1], *earlier[1:]], axis=0)
+        return jnp.roll(
+            arr_out, shift=(axis_index(mesh_ax) - n_blocks // 2) * matrix.shape[0], axis=0
+        )
+
+    columns = turn_modes(own_cols)
     complete = lax.all_gather(columns, "rep", axis=1, tiled=True)
     projected = jnp.dot(normed, complete, preferred_element_type=jnp.float32)
     projected = (projected + qkv_bias.astype(jnp.float32)).reshape(

time: 1130 us -> 1210 us (1.071); the launches traced: 1130 us -> 1200 us
  waiting for transfers between devices: 921 us -> 656 us
  starting transfers between devices: 3.13 us -> 246 us
  local copies, waits for them, and re-layouts: 53.4 us -> 148 us
    all_gather x1 -> x0, waiting for transfers between devices: 798 us -> none  [on_device(): columns = lax.all_gather(own_cols, 'grp', axis=0, tiled=True)]
    ppermute x0 -> x7, waiting for transfers between devices: none -> 552 us  [the longest x4 550 us: turn_modes(): mid_arr.append(ppermute(mid_arr[-1], axis_name=mesh_ax, perm=fields))]
    ppermute x0 -> x7, starting transfers between devices: none -> 241 us  [the longest x3 233 us: turn_modes(): earlier.append(ppermute(earlier[-1], axis_name=mesh_ax, perm=rows))]
    unnamed x32 -> x63, local copies, waits for them, and re-layouts: 22.7 us -> 87 us
    dynamic_slice x0 -> x1, local copies, waits for them, and re-layouts: none -> 29 us  [turn_modes(): jnp.roll(arr_out, shift=(axis_index(mesh_ax) - n_blocks // 2) * matrix.sh...]
    ppermute x2, waiting for transfers between devices: 27.4 us -> 11.7 us  [shifted(): return lax.ppermute(block, axis, route)]
  transfers between devices with their start and end apart: 4 -> 10, of which waited for: 3 -> 7; matrix products, arithmetic and copies ran while one was open for 7% -> 9% of each run, Pallas kernels for 0% -> 0%
where the time goes in v1:
time: 1210 us; the launch traced here: 1200 us
  waiting for transfers between devices  656 us (54%)
  starting transfers between devices  246 us (20%)
  local copies, waits for them, and re-layouts  148 us (12%)
  matrix products  95.3 us (8%)
  other arithmetic  34.4 us (3%)
  between operations  14.6 us (1%)
    ppermute x4, waiting for transfers between devices, turn_modes(): mid_arr.append(ppermute(mid_arr[-1], axis_name=mesh_ax, perm=fields))  550 us
    ppermute x3, starting transfers between devices, turn_modes(): earlier.append(ppermute(earlier[-1], axis_name=mesh_ax, perm=rows))  233 us
    all_gather x1, waiting for transfers between devices, on_device(): complete = lax.all_gather(columns, 'rep', axis=1, tiled=True)  92 us
    unnamed x63, local copies, waits for them, and re-layouts  87 us
    dot_general x1, matrix products, on_device(): projected = jnp.dot(normed, complete, preferred_element_type=jnp.float32)  47.7 us
    dynamic_slice x1, local copies, waits for them, and re-layouts, turn_modes(): jnp.roll(arr_out, shift=(axis_index(mesh_ax) - n_blocks // 2) * matrix.sh...  29 us
    sub x1, matrix products, on_device(): exponent = jnp.where(allowed, jnp.exp(scores - highest), 0.0)  24.2 us
  transfers between devices with their start and end apart: 10, of which 7 were waited for; matrix products, arithmetic and copies ran while one was open for 9% of the time, Pallas kernels for 0%

profile of v1, /device:TPU:0, one launch (start us, length us, event | category | flops | bytes accessed | tf_op | source)
XLA Modules:
  0.0 1199.0 jit_solution(7161930958652726977)
XLA Ops:
  13.1 116.1 %collective-permute-done = bf16[1024,2560]{1,0:T(8,128)(2,1)S(1)} collective-permute-done((bf16[1024,2560]{1,0:T(8,128)(2,1)S(1)}, bf16[1024,2560]{1,0:T(8,128)(2,1)S(1)}, u32[]{:S(2)}, u32[]{:S(2)}) %collective-permute-start) | collective-permute-done | bytes 5242912 | tf_op jit(solution)/shard_map/ppermute | solution.py:116
  136.2 219.6 %collective-permute-done.1 = bf16[1024,2560]{1,0:T(8,128)(2,1)S(1)} collective-permute-done((bf16[1024,2560]{1,0:T(8,128)(2,1)S(1)}, bf16[1024,2560]{1,0:T(8,128)(2,1)S(1)}, u32[]{:S(2)}, u32[]{:S(2)}) %collective-permute-start.1) | collective-permute-done | bytes 5242912 | tf_op jit(solution)/shard_map/ppermute | solution.py:116
  360.7 113.3 %collective-permute-start.5 = (bf16[1024,2560]{1,0:T(8,128)(2,1)S(1)}, bf16[1024,2560]{1,0:T(8,128)(2,1)}, u32[]{:S(2)}, u32[]{:S(2)}) collective-permute-start(bf16[1024,2560]{1,0:T(8,128)(2,1)S(1)} %collective-permute-done.4), channel_id=1, source_target_pairs={{0,28},{4,0},{8,4},{12,8},{16,12},{20,16},{24,20},{28,24},{1,29},{... | collective-permute-start | bytes 15728648 | tf_op jit(solution)/shard_map/ppermute | solution.py:118
  474.0 107.9 %collective-permute-done.2 = bf16[1024,2560]{1,0:T(8,128)(2,1)} collective-permute-done((bf16[1024,2560]{1,0:T(8,128)(2,1)S(1)}, bf16[1024,2560]{1,0:T(8,128)(2,1)}, u32[]{:S(2)}, u32[]{:S(2)}) %collective-permute-start.2) | collective-permute-done | bytes 5242912 | tf_op jit(solution)/shard_map/ppermute | solution.py:116
  586.5 114.8 %collective-permute-start.6 = (bf16[1024,2560]{1,0:T(8,128)(2,1)}, bf16[1024,2560]{1,0:T(8,128)(2,1)}, u32[]{:S(2)}, u32[]{:S(2)}) collective-permute-start(bf16[1024,2560]{1,0:T(8,128)(2,1)} %collective-permute-done.5), channel_id=1, source_target_pairs={{0,28},{4,0},{8,4},{12,8},{16,12},{20,16},{24,20},{28,24},{1,29},{... | collective-permute-start | bytes 15728648 | tf_op jit(solution)/shard_map/ppermute | solution.py:118
  701.4 106.3 %collective-permute-done.3 = bf16[1024,2560]{1,0:T(8,128)(2,1)} collective-permute-done((bf16[1024,2560]{1,0:T(8,128)(2,1)}, bf16[1024,2560]{1,0:T(8,128)(2,1)}, u32[]{:S(2)}, u32[]{:S(2)}) %collective-permute-start.3) | collective-permute-done | bytes 5242912 | tf_op jit(solution)/shard_map/ppermute | solution.py:116
  807.7 5.6 constant_dynamic-update-slice_fusion.15
  813.3 5.4 constant_dynamic-update-slice_fusion.14
  842.5 5.2 constant_dynamic-update-slice_fusion.7
  865.8 5.1 constant_dynamic-update-slice_fusion.1
  870.9 5.2 constant_dynamic-update-slice_fusion
  876.1 29.0 %constant_dynamic-slice_fusion = bf16[8192,2560]{1,0:T(8,128)(2,1)} fusion(bf16[16384,2560]{1,0:T(8,128)(2,1)} %constant_dynamic-update-slice_fusion, s32[]{:T(128)S(6)} %select_n.111), kind=kLoop, calls=%fused_computation.140 | loop fusion | bytes 83886080 | tf_op jit(solution)/shard_map/jit(_roll_dynamic)/dynamic_slice | solution.py:120
  910.7 6.1 fusion.9
  919.0 12.1 %fusion.11 = bf16[384,8192]{1,0:T(8,128)(2,1)} fusion(bf16[1,384,8192]{2,1,0:T(8,128)(2,1)} %param.6, f32[8192]{0:T(1024)S(1)} %convert_element_type.70, f32[384]{0:T(512)S(1)} %add_rsqrt_fusion), kind=kLoop, calls=%fused_computation.16 | loop fusion | flops 12582912 | bytes 12617216 | tf_op jit(solution)/shard_map/convert_element_type | solution.py:24
  931.1 92.0 %all-gather.3.cloned.1.call-done = bf16[8192,5120]{1,0:T(8,128)(2,1)} async-done(((bf16[8192,2560]{1,0:T(8,128)(2,1)}), bf16[8192,5120]{1,0:T(8,128)(2,1)}) %all-gather.3.cloned.1.call-update) | async-done | bytes 83886096 | tf_op jit(solution)/shard_map/all_gather | solution.py:125
  1023.2 47.7 %fusion.16 = f32[448,5120]{1,0:T(8,128)} fusion(bf16[8192,5120]{1,0:T(8,128)(2,1)} %all-gather.3.cloned.1.call-done, bf16[64,8192]{1,0:T(8,128)(2,1)S(1)} %fusion.32, bf16[384,8192]{1,0:T(8,128)(2,1)} %fusion.11, f32[5120]{0:T(1024)S(1)} %convert_element_type.76), kind=kOutput, calls=%fused_computation.24 | convolution fusion | flops 37597937664 | bytes 100421632 | tf_op jit(solution)/shard_map/dot_general | solution.py:126
  1070.8 11.0 copy.20
  1081.8 8.7 fusion.92
  1093.7 6.5 copy.56
  1100.2 6.5 copy.57
  1110.0 6.3 add_convert_fusion
  1129.9 24.2 %fusion.93 = (f32[4,8,384]{2,1,0:T(8,128)S(1)}, f32[4,8,384,768]{2,3,1,0:T(8,128)}) fusion(pred[384,768]{0,1:T(8,128)(4,1)S(1)} %copy-done.8, bf16[768,4,128]{2,0,1:T(8,128)(2,1)S(1)} %all_gather.11, bf16[448,4,8,64]{3,0,2,1:T(8,128)(2,1)} %copy-done.2, bf16[448,4,8,64]{3,0,2,1:T(8,128)(2,1)} %copy-done.1), kind=kOutput, calls=%fused_computation.156 | convolution fusion | flops 4901044736 | bytes 54640640 | tf_op jit(solution)/shard_map/sub | solution.py:160
  1154.2 15.2 %fusion.30 = bf16[4,128,8,384]{3,1,2,0:T(8,128)(2,1)} fusion(f32[4,8,384,768]{2,3,1,0:T(8,128)} %get-tuple-element.19, f32[4,8,384]{2,1,0:T(8,128)S(1)} %get-tuple-element.18, bf16[768,4,1,128]{0,3,1,2:T(8,128)(2,1)} %copy-done.7), kind=kOutput, calls=%fused_computation.45 | convolution fusion | flops 2436366336 | bytes 41730048 | tf_op jit(solution)/shard_map/aprk,kaz->rapz/dot_general | solution.py:49
  1176.9 11.7 collective-permute-done.7
  (121 shorter events, 102.7 us)
Async XLA Ops:
  7.2 1016.0 %all-gather.3.cloned.1.call-start = ((), (), s32[]{:S(2)}) async-start(), calls=%async_computation | async-start | bytes 125829120 | tf_op jit(solution)/shard_map/all_gather | solution.py:125
  10.0 119.1 %collective-permute-start = (bf16[1024,2560]{1,0:T(8,128)(2,1)S(1)}, bf16[1024,2560]{1,0:T(8,128)(2,1)S(1)}, u32[]{:S(2)}, u32[]{:S(2)}) collective-permute-start(bf16[1024,2560]{1,0:T(8,128)(2,1)S(1)} %constant_dynamic-slice_fusion.1), channel_id=1, source_target_pairs={{0,4},{4,8},{8,12},{12,16},{16,20},{20,24},{24,28},{28,0},{1,5},{5... | collective-permute-start | bytes 15728648 | tf_op jit(solution)/shard_map/ppermute | solution.py:116
  131.4 224.4 %collective-permute-start.1 = (bf16[1024,2560]{1,0:T(8,128)(2,1)S(1)}, bf16[1024,2560]{1,0:T(8,128)(2,1)S(1)}, u32[]{:S(2)}, u32[]{:S(2)}) collective-permute-start(bf16[1024,2560]{1,0:T(8,128)(2,1)S(1)} %collective-permute-done), channel_id=1, source_target_pairs={{0,4},{4,8},{8,12},{12,16},{16,20},{20,24},{24,28},{28,0},{1,5},{5... | collective-permute-start | bytes 15728648 | tf_op jit(solution)/shard_map/ppermute | solution.py:116
  131.4 226.8 %collective-permute-start.4 = (bf16[1024,2560]{1,0:T(8,128)(2,1)S(1)}, bf16[1024,2560]{1,0:T(8,128)(2,1)S(1)}, u32[]{:S(2)}, u32[]{:S(2)}) collective-permute-start(bf16[1024,2560]{1,0:T(8,128)(2,1)S(1)} %constant_dynamic-slice_fusion.1), channel_id=1, source_target_pairs={{0,28},{4,0},{8,4},{12,8},{16,12},{20,16},{24,20},{28,24},{1,29},{... | collective-permute-start | bytes 15728648 | tf_op jit(solution)/shard_map/ppermute | solution.py:118
  355.8 230.7 %copy-start.5 = (bf16[1024,2560]{1,0:T(8,128)(2,1)}, bf16[1024,2560]{1,0:T(8,128)(2,1)S(1)}, u32[]{:S(2)}) copy-start(bf16[1024,2560]{1,0:T(8,128)(2,1)S(1)} %collective-permute-done.1) | copy-start | bytes 15728644
  355.8 226.1 %collective-permute-start.2 = (bf16[1024,2560]{1,0:T(8,128)(2,1)S(1)}, bf16[1024,2560]{1,0:T(8,128)(2,1)}, u32[]{:S(2)}, u32[]{:S(2)}) collective-permute-start(bf16[1024,2560]{1,0:T(8,128)(2,1)S(1)} %collective-permute-done.1), channel_id=1, source_target_pairs={{0,4},{4,8},{8,12},{12,16},{16,20},{20,24},{24,28},{28,0},{1,5},{5... | collective-permute-start | bytes 15728648 | tf_op jit(solution)/shard_map/ppermute | solution.py:116
  360.7 225.8 %collective-permute-start.5 = (bf16[1024,2560]{1,0:T(8,128)(2,1)S(1)}, bf16[1024,2560]{1,0:T(8,128)(2,1)}, u32[]{:S(2)}, u32[]{:S(2)}) collective-permute-start(bf16[1024,2560]{1,0:T(8,128)(2,1)S(1)} %collective-permute-done.4), channel_id=1, source_target_pairs={{0,28},{4,0},{8,4},{12,8},{16,12},{20,16},{24,20},{28,24},{1,29},{... | collective-permute-start | bytes 15728648 | tf_op jit(solution)/shard_map/ppermute | solution.py:118
  582.0 225.7 %collective-permute-start.3 = (bf16[1024,2560]{1,0:T(8,128)(2,1)}, bf16[1024,2560]{1,0:T(8,128)(2,1)}, u32[]{:S(2)}, u32[]{:S(2)}) collective-permute-start(bf16[1024,2560]{1,0:T(8,128)(2,1)} %collective-permute-done.2), channel_id=1, source_target_pairs={{0,4},{4,8},{8,12},{12,16},{16,20},{20,24},{24,28},{28,0},{1,5},{5... | collective-permute-start | bytes 15728648 | tf_op jit(solution)/shard_map/ppermute | solution.py:116
  586.5 250.8 %collective-permute-start.6 = (bf16[1024,2560]{1,0:T(8,128)(2,1)}, bf16[1024,2560]{1,0:T(8,128)(2,1)}, u32[]{:S(2)}, u32[]{:S(2)}) collective-permute-start(bf16[1024,2560]{1,0:T(8,128)(2,1)} %collective-permute-done.5), channel_id=1, source_target_pairs={{0,28},{4,0},{8,4},{12,8},{16,12},{20,16},{24,20},{28,24},{1,29},{... | collective-permute-start | bytes 15728648 | tf_op jit(solution)/shard_map/ppermute | solution.py:118
  807.7 11.1 slice-start.7
  807.7 14.1 %slice-start.3 = ((s8[5242880]{0:T(1024)(128)(4,1)}), s8[4194304]{0:T(1024)(128)(4,1)S(1)}, s32[]{:S(2)}) async-start(s8[5242880]{0:T(1024)(128)(4,1)} %bitcast.154), calls=%async_computation.4 | async-start | bytes 8388608
  813.3 5.4 slice-start.8
  813.3 8.5 slice-start.4
  818.7 6.0 slice-start
  818.7 7.2 slice-start.1
  821.8 5.1 slice-start.2
  821.8 7.8 slice-start.5
  1081.8 8.7 copy-start
  1116.3 3.7 copy-start.1
  1116.3 3.7 copy-start.2
  1117.2 56.7 %collective-permute-start.8 = (bf16[768,4,128]{2,0,1:T(8,128)(2,1)S(1)}, bf16[768,4,128]{2,0,1:T(8,128)(2,1)S(1)}, u32[]{:S(2)}, u32[]{:S(2)}) collective-permute-start(bf16[768,4,128]{2,0,1:T(8,128)(2,1)S(1)} %all_gather.11), channel_id=1, source_target_pairs={{16,0},{20,4},{24,8},{28,12},{0,16},{4,20},{8,24},{12,28},{17,1},{... | collective-permute-start | bytes 2359304 | tf_op jit(solution)/shard_map/ppermute | solution.py:18
  1125.5 4.5 copy-start.8
  1128.0 60.7 %collective-permute-start.7 = (bf16[768,4,128]{0,2,1:T(8,128)(2,1)}, bf16[768,4,128]{0,2,1:T(8,128)(2,1)}, u32[]{:S(2)}, u32[]{:S(2)}) collective-permute-start(bf16[768,4,128]{0,2,1:T(8,128)(2,1)} %bitcast.162), channel_id=1, source_target_pairs={{16,0},{20,4},{24,8},{28,12},{0,16},{4,20},{8,24},{12,28},{17,1},{... | collective-permute-start | bytes 2359304 | tf_op jit(solution)/shard_map/ppermute | solution.py:18
  1169.4 4.6 copy-start.11
  (8 other events, 15.1 us)
Sparse Core Ops, SparseCore 0:
  905.2 117.8 all-gather.2
